TPU v7x, 32 devices: a whole 2x2x4 slice. The times are simulated.
32 devices in a mesh: dp: 4 (over x, core), expert: 8 (over z, y).
Axes of the slice: x: 2, y: 2, z: 4, core: 2. Of those that a mesh axis runs over, the one named last changes fastest.
Arguments:
- tokens: bfloat16 [4096, 4096], P(('dp', 'expert')), may hold values from -6 to 6
- expert_ids: int32 [4096, 2], P(('dp', 'expert')), may hold values from 0 to 7, as said below
- gate_codes: int32 [4096, 2], P(('dp', 'expert')), may hold values from 1 to 64
- w_gate: bfloat16 [8, 4096, 768], P('expert'), may hold values from -0.09375 to 0.09375
- w_up: bfloat16 [8, 4096, 768], P('expert'), may hold values from -0.09375 to 0.09375
- w_down: bfloat16 [8, 768, 4096], P('expert'), may hold values from -0.21875 to 0.21875
- out_grad: bfloat16 [4096, 4096], P(('dp', 'expert')), may hold values from -6 to 6
Outputs:
- layer_out: bfloat16 [4096, 4096], P(('dp', 'expert'))
- tokens_grad: bfloat16 [4096, 4096], P(('dp', 'expert'))
- gate_weight_grad: bfloat16 [8, 4096, 768], P('expert', 'dp')
- up_weight_grad: bfloat16 [8, 4096, 768], P('expert', 'dp')
- down_weight_grad: bfloat16 [8, 768, 4096], P('expert', None, 'dp')
Inputs may be any that keep to these rules, and one draw needn't show every extreme that they name: `expert_ids`: each token names 2 different experts. In the rows of one device no expert is named more than 48 times, and in every draw one and the same expert is named exactly 48 times by the rows of every device.
All inputs are finite; a program needn't handle non-finite values.
Results may differ from a plain program's by a relative error of at most 0.009.
Values may be sent and summed in bfloat16 or wider, within the bound.
A program may use at most 192 MiB of HBM per device.

v0:
```python
import jax
import jax.numpy as jnp
from jax import lax
from jax.sharding import PartitionSpec as P


def slot_targets(block_ids, experts, capacity):
    flat_ids = block_ids.reshape(-1)
    one_hot = (flat_ids[:, None] == jnp.arange(experts, dtype=jnp.int32)[None, :]).astype(jnp.int32)
    earlier = jnp.cumsum(one_hot, axis=0) - one_hot
    slot_ranks = jnp.sum(earlier * one_hot, axis=1)
    return flat_ids * capacity + slot_ranks


def per_device(tokens, expert_ids, gate_codes, w_gate, w_up, w_down, out_grad):
    experts = lax.axis_size("expert")
    tok_count, model_width = tokens.shape
    top_count = expert_ids.shape[1]
    pair_count = tok_count * top_count
    capacity = 3 * pair_count // (2 * experts)
    targets = slot_targets(expert_ids, experts, capacity)
    owners = (
        jnp.full((experts * capacity,), -1, jnp.int32)
        .at[targets]
        .set(jnp.arange(pair_count, dtype=jnp.int32))
    )
    is_live = owners >= 0
    safe_pair = jnp.maximum(owners, 0)
    token_pos = safe_pair // top_count
    gate_flat = gate_codes.astype(jnp.float32).reshape(-1) / 64.0
    pair_gains = jnp.where(is_live, gate_flat[safe_pair], 0.0)
    outbound = jnp.where(is_live[:, None], tokens[token_pos], jnp.zeros((), jnp.bfloat16))
    outbound = outbound.reshape(experts, capacity, model_width)
    gate_matrix = w_gate[0]
    up_matrix = w_up[0]
    down_matrix = w_down[0]
    hidden_units = gate_matrix.shape[1]
    contract = (((1,), (1,)), ((), ()))
    contract_rows = (((0,), (0,)), ((), ()))
    received = lax.all_to_all(outbound, "expert", split_axis=0, concat_axis=0, tiled=True)
    slot_count = received.shape[1]
    expert_row_block = received.reshape(-1, model_width)
    pre_gate = jnp.dot(expert_row_block, gate_matrix, preferred_element_type=jnp.float32)
    pre_up = jnp.dot(expert_row_block, up_matrix, preferred_element_type=jnp.float32)
    expert_hidden = (pre_gate * jax.nn.sigmoid(pre_gate) * pre_up).astype(jnp.bfloat16)
    produced = jnp.dot(expert_hidden, down_matrix, preferred_element_type=jnp.float32).astype(
        jnp.bfloat16
    )
    produced = produced.reshape(experts, slot_count, model_width)
    returned = lax.all_to_all(produced, "expert", split_axis=0, concat_axis=0, tiled=True)
    returned, arrived, pre_gate, pre_up, hidden = (
        returned,
        received,
        pre_gate.reshape(experts, slot_count, hidden_units),
        pre_up.reshape(experts, slot_count, hidden_units),
        expert_hidden.reshape(experts, slot_count, hidden_units),
    )
    pair_out = returned.reshape(-1, model_width)[targets].astype(jnp.float32)
    weighted = gate_flat[:, None] * pair_out
    layer_out = jnp.sum(weighted.reshape(tok_count, top_count, model_width), axis=1).astype(
        jnp.bfloat16
    )
    upstream = out_grad[token_pos]
    pair_grad = (pair_gains[:, None] * upstream.astype(jnp.float32)).astype(jnp.bfloat16)
    pair_grad = pair_grad.reshape(experts, capacity, model_width)
    incoming = lax.all_to_all(pair_grad, "expert", split_axis=0, concat_axis=0, tiled=True).reshape(
        -1, model_width
    )
    pre_gate = pre_gate.reshape(-1, hidden_units)
    pre_up = pre_up.reshape(-1, hidden_units)
    hidden = hidden.reshape(-1, hidden_units)
    sigmoid_gate = jax.nn.sigmoid(pre_gate)
    silu_gate = pre_gate * sigmoid_gate
    hidden_grad = lax.dot_general(
        incoming, down_matrix, contract, preferred_element_type=jnp.float32
    )
    gate_pre_grad = (
        hidden_grad * pre_up * sigmoid_gate * (1.0 + pre_gate * (1.0 - sigmoid_gate))
    ).astype(jnp.bfloat16)
    up_pre_grad = (hidden_grad * silu_gate).astype(jnp.bfloat16)
    input_grad = lax.dot_general(
        gate_pre_grad, gate_matrix, contract, preferred_element_type=jnp.float32
    )
    input_grad = input_grad + lax.dot_general(
        up_pre_grad, up_matrix, contract, preferred_element_type=jnp.float32
    )
    input_grad = input_grad.astype(jnp.bfloat16).reshape(experts, capacity, model_width)
    returned_grad = lax.all_to_all(input_grad, "expert", split_axis=0, concat_axis=0, tiled=True)
    pair_input = returned_grad.reshape(-1, model_width)[targets].astype(jnp.float32)
    tokens_grad = jnp.sum(pair_input.reshape(tok_count, top_count, model_width), axis=1).astype(
        jnp.bfloat16
    )
    row_block = arrived.reshape(-1, model_width)
    column_block = row_block
    gate_sum = lax.psum_scatter(
        lax.dot_general(
            column_block, gate_pre_grad, contract_rows, preferred_element_type=jnp.float32
        ).astype(jnp.bfloat16),
        "dp",
        scatter_dimension=0,
        tiled=True,
    )
    column_block = row_block
    up_sum = lax.psum_scatter(
        lax.dot_general(
            column_block, up_pre_grad, contract_rows, preferred_element_type=jnp.float32
        ).astype(jnp.bfloat16),
        "dp",
        scatter_dimension=0,
        tiled=True,
    )
    column_block = incoming
    down_sum = (
        lax.psum_scatter(
            lax.dot_general(
                column_block, hidden, contract_rows, preferred_element_type=jnp.float32
            ).astype(jnp.bfloat16),
            "dp",
            scatter_dimension=0,
            tiled=True,
        )
        .astype(jnp.float32)
        .T
    )
    return (
        layer_out,
        tokens_grad,
        gate_sum[None],
        up_sum[None],
        down_sum.astype(jnp.bfloat16)[None],
    )


def solution(mesh):
    placed = (
        P(("dp", "expert"), None),
        P(("dp", "expert"), None),
        P(("dp", "expert"), None),
        P("expert", None, None),
        P("expert", None, None),
        P("expert", None, None),
        P(("dp", "expert"), None),
    )
    return jax.shard_map(
        per_device,
        mesh=mesh,
        in_specs=placed,
        out_specs=(
            P(("dp", "expert"), None),
            P(("dp", "expert"), None),
            P("expert", "dp", None),
            P("expert", "dp", None),
            P("expert", None, "dp"),
        ),
        check_vma=False,
    )
```

profile of v0, /device:TPU:0, one launch (start us, length us, event | category | flops | bytes accessed | tf_op | source)
XLA Modules:
  0.0 404.6 jit_solution(15272280271444568787)
XLA Ops:
  7.2 0.0 copy-start
  7.2 0.8 broadcast_multiply_fusion
  8.0 0.8 copy.16
  8.7 0.1 eq.29
  8.9 0.1 eq.25
  9.0 0.7 convert_multiply_fusion.1
  9.7 0.1 copy.14
  9.8 0.1 div.22
  10.0 0.1 copy.15
  10.1 0.1 mul.64
  10.2 0.6 reduce-window.6
  10.8 0.2 slice_reduce_fusion
  11.1 0.1 fusion.20
  11.2 1.4 scatter_custom_fusion
  12.6 2.8 gather_fusion.2
  15.5 0.1 mul.69
  15.5 0.0 copy-done
  15.5 4.1 %gather_fusion.3 = bf16[384,4096]{1,0:T(8,128)(2,1)} fusion(bf16[128,4096]{1,0:T(8,128)(2,1)S(1)} %copy-done, s32[1024]{0:T(1024)S(1)} %get-tuple-element.23), kind=kCustom, calls=%fused_computation.3 | custom fusion | bytes 6292992 | tf_op jit(solution)/shard_map/gather | solution.py:63
  19.6 4.6 %fusion = bf16[8,48,4096]{2,1,0:T(8,128)(2,1)} fusion(bf16[8,48,4096]{2,1,0:T(8,128)(2,1)} %bitcast.60, f32[8,48]{1,0:T(8,128)S(1)} %mul.69), kind=kLoop, calls=%fused_computation.10 | loop fusion | flops 4718592 | bytes 6292992 | tf_op jit(solution)/shard_map/convert_element_type | solution.py:64
  24.2 0.0 copy-start.2
  24.2 7.4 %all-to-all-start.2 = ((bf16[8,48,4096]{2,1,0:T(8,128)(2,1)}), bf16[8,48,4096]{2,1,0:T(8,128)(2,1)}, u32[]{:S(2)}, u32[]{:S(2)}) async-start(bf16[8,48,4096]{2,1,0:T(8,128)(2,1)} %fusion), calls=%async_computation.2 | async-start | bytes 6291456 | tf_op jit(solution)/shard_map/all_to_all | solution.py:66
  31.6 0.1 broadcast_in_dim.45
  31.7 0.0 copy-done.2
  31.7 4.0 gather_fusion
  35.7 3.9 broadcast_select_fusion
  39.6 62.8 %all-to-all-done.2 = bf16[8,48,4096]{2,1,0:T(8,128)(2,1)} async-done(((bf16[8,48,4096]{2,1,0:T(8,128)(2,1)}), bf16[8,48,4096]{2,1,0:T(8,128)(2,1)}, u32[]{:S(2)}, u32[]{:S(2)}) %all-to-all-start.2) | async-done | bytes 3145760 | tf_op jit(solution)/shard_map/all_to_all | solution.py:66
  102.4 3.6 all-to-all-start
  106.1 0.5 reduce-scatter.8.cloned.1.call-start
  106.6 7.4 %fusion.1 = f32[384,768]{1,0:T(8,128)} fusion(bf16[384,4096]{1,0:T(8,128)(2,1)} %bitcast.12, bf16[1,768,4096]{2,1,0:T(8,128)(2,1)} %param.12), kind=kOutput, calls=%fused_computation.11 | convolution fusion | flops 2415919104 | bytes 10616832 | tf_op jit(solution)/shard_map/dot_general | solution.py:74
  114.0 63.0 %all-to-all-done = bf16[8,48,4096]{2,1,0:T(8,128)(2,1)S(1)} async-done(((bf16[8,48,4096]{2,1,0:T(8,128)(2,1)}), bf16[8,48,4096]{2,1,0:T(8,128)(2,1)S(1)}, u32[]{:S(2)}, u32[]{:S(2)}) %all-to-all-start) | async-done | bytes 3145760 | tf_op jit(solution)/shard_map/all_to_all | solution.py:40
  176.9 0.0 copy-start.6
  176.9 5.5 %fusion.7 = f32[384,768]{1,0:T(8,128)S(1)} fusion(bf16[384,4096]{1,0:T(8,128)(2,1)S(1)} %bitcast.61, bf16[1,4096,768]{2,1,0:T(8,128)(2,1)} %param.11), kind=kOutput, calls=%fused_computation.17 | convolution fusion | flops 2415919104 | bytes 10616832 | tf_op jit(solution)/shard_map/dot_general | solution.py:44
  182.4 0.0 copy-done.6
  182.4 6.8 %multiply_convert_fusion.1 = (bf16[384,768]{1,0:T(8,128)(2,1)}, bf16[384,768]{1,0:T(8,128)(2,1)}, bf16[384,768]{1,0:T(8,128)(2,1)S(1)}) fusion(f32[384,768]{1,0:T(8,128)S(1)} %copy-done.6, f32[384,768]{1,0:T(8,128)S(1)} %fusion.7, bf16[384,4096]{1,0:T(8,128)(2,1)S(1)} %bitcast.62, bf16[1,4096,768]{2,1,0:T(8,128)(2,1)} %param.10), kind=kOutput, calls=%fused_computation.28 | convolution fusion | flops 2420342784 | bytes 13565952 | tf_op jit(solution)/shard_map/dot_general | solution.py:43
  189.2 0.0 copy-start.4
  189.2 0.8 copy-done.4
  190.0 8.0 %convolution_convert_fusion = bf16[4096,768]{1,0:T(8,128)(2,1)} fusion(bf16[384,4096]{1,0:T(8,128)(2,1)} %bitcast.12, bf16[384,768]{1,0:T(8,128)(2,1)S(1)} %get-tuple-element.19), kind=kOutput, calls=%fused_computation.6 | convolution fusion | flops 2419064832 | bytes 10027008 | tf_op jit(solution)/shard_map/dot_general | solution.py:115
  198.1 0.0 reduce-scatter.8.cloned.1.call-update
  198.1 0.0 reduce-scatter.4.cloned.1.call-start
  198.1 6.4 %convolution_convert_fusion.2 = bf16[4096,768]{1,0:T(8,128)(2,1)} fusion(bf16[384,4096]{1,0:T(8,128)(2,1)S(1)} %bitcast.63, bf16[384,768]{1,0:T(8,128)(2,1)} %get-tuple-element.17), kind=kOutput, calls=%fused_computation.8 | convolution fusion | flops 2419064832 | bytes 10027008 | tf_op jit(solution)/shard_map/dot_general | solution.py:96
  204.5 0.0 reduce-scatter.4.cloned.1.call-update
  204.6 0.2 reduce-scatter.6.cloned.1.call-start
  204.8 6.7 %convolution_convert_fusion.1 = bf16[4096,768]{1,0:T(8,128)(2,1)} fusion(bf16[384,4096]{1,0:T(8,128)(2,1)S(1)} %bitcast.64, bf16[384,768]{1,0:T(8,128)(2,1)} %get-tuple-element.18), kind=kOutput, calls=%fused_computation.7 | convolution fusion | flops 2419064832 | bytes 10027008 | tf_op jit(solution)/shard_map/dot_general | solution.py:105
  211.4 0.0 copy-start.5
  211.4 0.0 reduce-scatter.6.cloned.1.call-update
  211.5 1.0 copy-done.5
  212.5 6.8 %fusion.15 = bf16[384,4096]{1,0:T(8,128)(2,1)} fusion(bf16[384,768]{1,0:T(8,128)(2,1)S(1)} %copy-done.5, bf16[1,768,4096]{2,1,0:T(8,128)(2,1)} %param.12), kind=kOutput, calls=%fused_computation.24 | convolution fusion | flops 2417491968 | bytes 10027008 | tf_op jit(solution)/shard_map/dot_general | solution.py:46
  219.3 3.7 all-to-all-start.1
  223.0 0.0 copy-start.3
  223.0 4.9 %fusion.5 = f32[384,4096]{1,0:T(8,128)S(1)} fusion(bf16[384,768]{1,0:T(8,128)(2,1)} %get-tuple-element.18, bf16[1,4096,768]{2,1,0:T(8,128)(2,1)} %param.11), kind=kOutput, calls=%fused_computation.15 | convolution fusion | flops 2415919104 | bytes 13172736 | tf_op jit(solution)/shard_map/dot_general | solution.py:84
  227.9 0.0 copy-done.3
  227.9 8.5 %add_convert_fusion = bf16[384,4096]{1,0:T(8,128)(2,1)} fusion(f32[384,4096]{1,0:T(8,128)S(1)} %fusion.5, bf16[384,768]{1,0:T(8,128)(2,1)S(1)} %copy-done.3, bf16[1,4096,768]{2,1,0:T(8,128)(2,1)} %param.10), kind=kOutput, calls=%fused_computation.23 | convolution fusion | flops 2419064832 | bytes 16318464 | tf_op jit(solution)/shard_map/dot_general | solution.py:81
  236.5 57.5 %all-to-all-done.1 = bf16[8,48,4096]{2,1,0:T(8,128)(2,1)S(1)} async-done(((bf16[8,48,4096]{2,1,0:T(8,128)(2,1)}), bf16[8,48,4096]{2,1,0:T(8,128)(2,1)S(1)}, u32[]{:S(2)}, u32[]{:S(2)}) %all-to-all-start.1) | async-done | bytes 3145760 | tf_op jit(solution)/shard_map/all_to_all | solution.py:50
  294.0 4.4 %all-to-all-start.3 = ((bf16[8,48,4096]{2,1,0:T(8,128)(2,1)}), bf16[8,48,4096]{2,1,0:T(8,128)(2,1)}, u32[]{:S(2)}, u32[]{:S(2)}) async-start(bf16[8,48,4096]{2,1,0:T(8,128)(2,1)} %bitcast.65), calls=%async_computation.3 | async-start | bytes 6291456 | tf_op jit(solution)/shard_map/all_to_all | solution.py:88
  298.4 3.2 gather_fusion.1
  301.6 5.5 %reshape.118 = f32[128,2,4096]{2,1,0:T(2,128)} reshape(bf16[256,4096]{1,0:T(8,128)(2,1)} %gather_fusion.1) | data formatting | bytes 6291456 | tf_op jit(solution)/shard_map/convert_element_type | solution.py:58
  307.1 61.5 %all-to-all-done.3 = bf16[8,48,4096]{2,1,0:T(8,128)(2,1)} async-done(((bf16[8,48,4096]{2,1,0:T(8,128)(2,1)}), bf16[8,48,4096]{2,1,0:T(8,128)(2,1)}, u32[]{:S(2)}, u32[]{:S(2)}) %all-to-all-start.3) | async-done | bytes 3145760 | tf_op jit(solution)/shard_map/all_to_all | solution.py:88
  368.6 6.2 %gather_fusion.4 = bf16[256,4096]{1,0:T(8,128)(2,1)S(1)} fusion(bf16[384,4096]{1,0:T(8,128)(2,1)} %bitcast.14, s32[1024]{0:T(1024)S(1)} %pad_clamp_fusion.1), kind=kCustom, calls=%fused_computation.4 | custom fusion | bytes 4195328 | tf_op jit(solution)/shard_map/gather | solution.py:89
  374.8 2.9 gather.25
  377.7 0.0 copy-start.1
  377.7 7.9 %reduce_sum.35 = bf16[128,4096]{1,0:T(8,128)(2,1)} reduce(bf16[128,2,4096]{2,1,0:T(2,128)(2,1)} %gather.25, bf16[]{:T(256)} %constant.39.clone.1), dimensions={1}, to_apply=%region_5.6 | reduce | flops 524288 | bytes 3145730 | tf_op jit(solution)/shard_map/reduce_sum | solution.py:90
  385.6 9.6 %multiply_reduce_fusion = bf16[128,4096]{1,0:T(8,128)(2,1)} fusion(f32[128,2,4096]{2,1,0:T(2,128)} %reshape.118, f32[128,2]{1,0:T(8,128)S(1)} %copy.14), kind=kLoop, calls=%fused_computation.25 | loop fusion | flops 1572864 | bytes 5243904 | tf_op jit(solution)/shard_map/reduce_sum | solution.py:60
  395.2 2.6 copy.19
  397.8 0.0 copy-done.1
  (12 shorter events, 0.1 us)
Async XLA Ops:
  7.2 8.4 %copy-start = (bf16[128,4096]{1,0:T(8,128)(2,1)S(1)}, bf16[128,4096]{1,0:T(8,128)(2,1)}, u32[]{:S(2)}) copy-start(bf16[128,4096]{1,0:T(8,128)(2,1)} %param.13) | copy-start | bytes 3145732
  24.2 7.5 %copy-start.2 = (bf16[128,4096]{1,0:T(8,128)(2,1)S(1)}, bf16[128,4096]{1,0:T(8,128)(2,1)}, u32[]{:S(2)}) copy-start(bf16[128,4096]{1,0:T(8,128)(2,1)} %param.7) | copy-start | bytes 3145732
  24.2 78.2 %all-to-all-start.2 = ((bf16[8,48,4096]{2,1,0:T(8,128)(2,1)}), bf16[8,48,4096]{2,1,0:T(8,128)(2,1)}, u32[]{:S(2)}, u32[]{:S(2)}) async-start(bf16[8,48,4096]{2,1,0:T(8,128)(2,1)} %fusion), calls=%async_computation.2 | async-start | bytes 6291456 | tf_op jit(solution)/shard_map/all_to_all | solution.py:66
  102.4 74.5 %all-to-all-start = ((bf16[8,48,4096]{2,1,0:T(8,128)(2,1)}), bf16[8,48,4096]{2,1,0:T(8,128)(2,1)S(1)}, u32[]{:S(2)}, u32[]{:S(2)}) async-start(bf16[8,48,4096]{2,1,0:T(8,128)(2,1)} %broadcast_select_fusion), calls=%async_computation | async-start | bytes 6291456 | tf_op jit(solution)/shard_map/all_to_all | solution.py:40
  106.1 289.1 %reduce-scatter.8.cloned.1.call-start = ((), (), s32[]{:S(2)}) async-start(), calls=%async_computation.9 | async-start | bytes 7864320 | tf_op jit(solution)/shard_map/reduce_scatter | solution.py:114
  176.9 5.5 %copy-start.6 = (f32[384,768]{1,0:T(8,128)S(1)}, f32[384,768]{1,0:T(8,128)}, u32[]{:S(2)}) copy-start(f32[384,768]{1,0:T(8,128)} %fusion.1) | copy-start | bytes 3538948
  189.2 0.8 copy-start.4
  198.1 199.7 %reduce-scatter.4.cloned.1.call-start = ((), (), s32[]{:S(2)}) async-start(), calls=%async_computation.7 | async-start | bytes 7864320 | tf_op jit(solution)/shard_map/reduce_scatter | solution.py:95
  204.6 193.2 %reduce-scatter.6.cloned.1.call-start = ((), (), s32[]{:S(2)}) async-start(), calls=%async_computation.8 | async-start | bytes 7864320 | tf_op jit(solution)/shard_map/reduce_scatter | solution.py:104
  211.4 1.1 copy-start.5
  219.3 74.7 %all-to-all-start.1 = ((bf16[8,48,4096]{2,1,0:T(8,128)(2,1)}), bf16[8,48,4096]{2,1,0:T(8,128)(2,1)S(1)}, u32[]{:S(2)}, u32[]{:S(2)}) async-start(bf16[8,48,4096]{2,1,0:T(8,128)(2,1)} %bitcast.66), calls=%async_computation.1 | async-start | bytes 6291456 | tf_op jit(solution)/shard_map/all_to_all | solution.py:50
  223.0 5.0 %copy-start.3 = (bf16[384,768]{1,0:T(8,128)(2,1)S(1)}, bf16[384,768]{1,0:T(8,128)(2,1)}, u32[]{:S(2)}) copy-start(bf16[384,768]{1,0:T(8,128)(2,1)} %get-tuple-element.17) | copy-start | bytes 1769476
  294.0 74.6 %all-to-all-start.3 = ((bf16[8,48,4096]{2,1,0:T(8,128)(2,1)}), bf16[8,48,4096]{2,1,0:T(8,128)(2,1)}, u32[]{:S(2)}, u32[]{:S(2)}) async-start(bf16[8,48,4096]{2,1,0:T(8,128)(2,1)} %bitcast.65), calls=%async_computation.3 | async-start | bytes 6291456 | tf_op jit(solution)/shard_map/all_to_all | solution.py:88
  377.7 20.1 %copy-start.1 = (bf16[128,4096]{1,0:T(8,128)(2,1)S(1)}, bf16[128,4096]{1,0:T(8,128)(2,1)}, u32[]{:S(2)}) copy-start(bf16[128,4096]{1,0:T(8,128)(2,1)} %param.13) | copy-start | bytes 3145732
Sparse Core Ops, SparseCore 0:
  198.2 57.3 reduce-scatter.7
  258.9 58.3 reduce-scatter.3
  320.4 58.3 reduce-scatter.5
where the time goes:
time: 410 us; the launch traced here: 405 us
  waiting for transfers between devices  245 us (60%)
  matrix products  61 us (15%)
  local copies, waits for them, and re-layouts  36.4 us (9%)
  other arithmetic  28.2 us (7%)
  starting transfers between devices  20 us (5%)
  between operations  14.2 us (3%)
    all_to_all x1, waiting for transfers between devices, per_device(): lax.all_to_all(outbound, 'expert', split_axis=0, concat_axis=0, tiled=True)  63 us
    all_to_all x1, waiting for transfers between devices, per_device(): lax.all_to_all(pair_grad, 'expert', split_axis=0, concat_axis=0, tiled=True)  62.8 us
    all_to_all x1, waiting for transfers between devices, per_device(): lax.all_to_all(input_grad, 'expert', split_axis=0, concat_axis=0, tiled=T...  61.5 us
    all_to_all x1, waiting for transfers between devices, per_device(): lax.all_to_all(produced, 'expert', split_axis=0, concat_axis=0, tiled=True)  57.5 us
    reduce_sum x1, other arithmetic, per_device(): jnp.sum(weighted.reshape(tok_count, top_count, model_width), axis=1)  9.64 us
    gather x2, local copies, waits for them, and re-layouts, per_device(): returned_grad.reshape(-1, model_width)[targets].astype(jnp.float32)  9.04 us
    dot_general x1, matrix products, per_device(): lax.dot_general(gate_pre_grad, gate_matrix, contract, preferred_element_t...  8.54 us
  transfers between devices with their start and end apart: 7, of which 4 were waited for; matrix products, arithmetic and copies ran while one was open for 21% of the time, Pallas kernels for 0%

commit v1 on v0

--- a/solution.py
+++ b/solution.py
@@ -2,6 +2,29 @@
 import jax.numpy as jnp
 from jax import lax
 from jax.sharding import PartitionSpec as P
+
+
+def split_up(x, dim, peers):
+    dims = x.shape
+    tiles = x.reshape(*dims[:dim], peers, dims[dim] // peers, *dims[dim + 1 :])
+    return jnp.moveaxis(tiles, dim, 0)
+
+
+def laid_out(blocks, dim):
+    shape = list(blocks.shape[1:])
+    shape[dim] *= blocks.shape[0]
+    return jnp.moveaxis(blocks, 0, dim).reshape(shape)
+
+
+def exchange_directly(array, axis, split_dim, concat_dim):
+    devices, index = (lax.axis_size(axis), lax.axis_index(axis))
+    pieces = split_up(array, split_dim, devices)
+    outs = [pieces[index]]
+    for lap in range(1, devices):
+        sent = pieces[(index + lap) % devices]
+        outs.append(lax.ppermute(sent, axis, [(i, (i + lap) % devices) for i in range(devices)]))
+    pieces = jnp.stack(outs)[(index - jnp.arange(devices)) % devices]
+    return laid_out(pieces, concat_dim)
 
 
 def slot_targets(block_ids, experts, capacity):
@@ -85,7 +108,7 @@
         up_pre_grad, up_matrix, contract, preferred_element_type=jnp.float32
     )
     input_grad = input_grad.astype(jnp.bfloat16).reshape(experts, capacity, model_width)
-    returned_grad = lax.all_to_all(input_grad, "expert", split_axis=0, concat_axis=0, tiled=True)
+    returned_grad = exchange_directly(input_grad, "expert", 0, 0)
     pair_input = returned_grad.reshape(-1, model_width)[targets].astype(jnp.float32)
     tokens_grad = jnp.sum(pair_input.reshape(tok_count, top_count, model_width), axis=1).astype(
         jnp.bfloat16

time: 410 us -> 439 us (1.071)
  starting transfers between devices: 20 us -> 39.9 us
  local copies, waits for them, and re-layouts: 36.4 us -> 52.4 us
  waiting for transfers between devices: 245 us -> 237 us
    ppermute x0 -> x7, waiting for transfers between devices: none -> 112 us  [exchange_directly(): lax.ppermute(sent, axis, [(i, (i + lap) % devices) for i in range(devices)])]
    all_to_all x1 -> x0, waiting for transfers between devices: 61.5 us -> none  [per_device(): lax.all_to_all(input_grad, 'expert', split_axis=0, concat_axis=0, tiled=T...]
    all_to_all x1, waiting for transfers between devices: 57.5 us -> 0.01 us  [per_device(): lax.all_to_all(produced, 'expert', split_axis=0, concat_axis=0, tiled=True)]
    ppermute x0 -> x7, starting transfers between devices: none -> 23.4 us  [exchange_directly(): lax.ppermute(sent, axis, [(i, (i + lap) % devices) for i in range(devices)])]
    unnamed x16 -> x32, local copies, waits for them, and re-layouts: 5.24 us -> 10.8 us
    all_to_all x1 -> x0, starting transfers between devices: 4.45 us -> none  [per_device(): lax.all_to_all(input_grad, 'expert', split_axis=0, concat_axis=0, tiled=T...]
  transfers between devices with their start and end apart: 7 -> 13, of which waited for: 4 -> 5; matrix products, arithmetic and copies ran while one was open for 21% -> 23% of each run, Pallas kernels for 0% -> 0%
where the time goes in v1:
time: 439 us; the launch traced here: 431 us
  waiting for transfers between devices  237 us (54%)
  matrix products  58.7 us (13%)
  local copies, waits for them, and re-layouts  52.4 us (12%)
  starting transfers between devices  39.9 us (9%)
  other arithmetic  27.9 us (6%)
  between operations  14.3 us (3%)
    ppermute x7, waiting for transfers between devices, exchange_directly(): lax.ppermute(sent, axis, [(i, (i + lap) % devices) for i in range(devices)])  112 us
    all_to_all x1, waiting for transfers between devices, per_device(): lax.all_to_all(outbound, 'expert', split_axis=0, concat_axis=0, tiled=True)  62.9 us
    all_to_all x1, waiting for transfers between devices, per_device(): lax.all_to_all(pair_grad, 'expert', split_axis=0, concat_axis=0, tiled=True)  62.8 us
    ppermute x7, starting transfers between devices, exchange_directly(): lax.ppermute(sent, axis, [(i, (i + lap) % devices) for i in range(devices)])  23.4 us
    gather x2, local copies, waits for them, and re-layouts, per_device(): returned_grad.reshape(-1, model_width)[targets].astype(jnp.float32)  12.2 us
    unnamed x32, local copies, waits for them, and re-layouts  10.8 us
    reduce_sum x1, other arithmetic, per_device(): jnp.sum(weighted.reshape(tok_count, top_count, model_width), axis=1)  9.64 us
    dot_general x1, matrix products, per_device(): lax.dot_general(up_pre_grad, up_matrix, contract, preferred_element_type=...  8.97 us
  transfers between devices with their start and end apart: 13, of which 5 were waited for; matrix products, arithmetic and copies ran while one was open for 23% of the time, Pallas kernels for 0%

profile of v1, /device:TPU:0, one launch (start us, length us, event | category | flops | bytes accessed | tf_op | source)
XLA Modules:
  0.0 430.7 jit_solution(3980607539644316753)
XLA Ops:
  7.2 0.8 broadcast_multiply_fusion
  8.0 0.8 copy.16
  8.7 0.1 eq.39
  8.9 0.1 eq.35
  9.0 0.7 convert_multiply_fusion.1
  9.7 0.1 copy.14
  9.8 0.1 div.22
  10.0 0.1 copy.15
  10.1 0.1 mul.64
  10.2 0.6 reduce-window.6
  10.8 0.2 slice_reduce_fusion
  11.1 0.1 fusion.20
  11.2 1.4 scatter_custom_fusion
  12.6 2.8 gather_fusion.2
  15.5 0.1 mul.69
  15.5 4.1 gather_fusion.3
  19.6 4.5 %fusion = bf16[8,48,4096]{2,1,0:T(8,128)(2,1)} fusion(bf16[8,48,4096]{2,1,0:T(8,128)(2,1)} %bitcast.92, f32[8,48]{1,0:T(8,128)S(1)} %mul.69), kind=kLoop, calls=%fused_computation.11 | loop fusion | flops 4718592 | bytes 6292992 | tf_op jit(solution)/shard_map/convert_element_type | solution.py:87
  24.1 7.4 %all-to-all-start.2 = ((bf16[8,48,4096]{2,1,0:T(8,128)(2,1)}), bf16[8,48,4096]{2,1,0:T(8,128)(2,1)}, u32[]{:S(2)}, u32[]{:S(2)}) async-start(bf16[8,48,4096]{2,1,0:T(8,128)(2,1)} %fusion), calls=%async_computation.2 | async-start | bytes 6291456 | tf_op jit(solution)/shard_map/all_to_all | solution.py:89
  31.6 0.1 broadcast_in_dim.46
  31.6 4.1 gather_fusion
  35.7 3.8 broadcast_select_fusion
  39.5 62.8 %all-to-all-done.2 = bf16[8,48,4096]{2,1,0:T(8,128)(2,1)} async-done(((bf16[8,48,4096]{2,1,0:T(8,128)(2,1)}), bf16[8,48,4096]{2,1,0:T(8,128)(2,1)}, u32[]{:S(2)}, u32[]{:S(2)}) %all-to-all-start.2) | async-done | bytes 3145760 | tf_op jit(solution)/shard_map/all_to_all | solution.py:89
  102.4 3.6 all-to-all-start
  106.0 0.6 reduce-scatter.8.cloned.1.call-start
  106.6 7.4 %fusion.1 = f32[384,768]{1,0:T(8,128)} fusion(bf16[384,4096]{1,0:T(8,128)(2,1)} %bitcast.12, bf16[1,768,4096]{2,1,0:T(8,128)(2,1)} %param.12), kind=kOutput, calls=%fused_computation.12 | convolution fusion | flops 2415919104 | bytes 10616832 | tf_op jit(solution)/shard_map/dot_general | solution.py:97
  114.0 62.9 %all-to-all-done = bf16[8,48,4096]{2,1,0:T(8,128)(2,1)S(1)} async-done(((bf16[8,48,4096]{2,1,0:T(8,128)(2,1)}), bf16[8,48,4096]{2,1,0:T(8,128)(2,1)S(1)}, u32[]{:S(2)}, u32[]{:S(2)}) %all-to-all-start) | async-done | bytes 3145760 | tf_op jit(solution)/shard_map/all_to_all | solution.py:63
  176.9 5.5 %fusion.7 = f32[384,768]{1,0:T(8,128)S(1)} fusion(bf16[384,4096]{1,0:T(8,128)(2,1)S(1)} %bitcast.95, bf16[1,4096,768]{2,1,0:T(8,128)(2,1)} %param.11), kind=kOutput, calls=%fused_computation.18 | convolution fusion | flops 2415919104 | bytes 10616832 | tf_op jit(solution)/shard_map/dot_general | solution.py:67
  182.4 6.8 %multiply_convert_fusion.1 = (bf16[384,768]{1,0:T(8,128)(2,1)}, bf16[384,768]{1,0:T(8,128)(2,1)}, bf16[384,768]{1,0:T(8,128)(2,1)S(1)}) fusion(f32[384,768]{1,0:T(8,128)S(1)} %copy-done.7, f32[384,768]{1,0:T(8,128)S(1)} %fusion.7, bf16[384,4096]{1,0:T(8,128)(2,1)S(1)} %bitcast.96, bf16[1,4096,768]{2,1,0:T(8,128)(2,1)} %param.10), kind=kOutput, calls=%fused_computation.29 | convolution fusion | flops 2420342784 | bytes 13565952 | tf_op jit(solution)/shard_map/dot_general | solution.py:66
  189.2 0.8 copy-done.4
  190.0 8.0 %convolution_convert_fusion = bf16[4096,768]{1,0:T(8,128)(2,1)} fusion(bf16[384,4096]{1,0:T(8,128)(2,1)} %bitcast.12, bf16[384,768]{1,0:T(8,128)(2,1)S(1)} %get-tuple-element.27), kind=kOutput, calls=%fused_computation.7 | convolution fusion | flops 2419064832 | bytes 10027008 | tf_op jit(solution)/shard_map/dot_general | solution.py:138
  198.0 0.0 reduce-scatter.8.cloned.1.call-update
  198.0 0.0 reduce-scatter.4.cloned.1.call-start
  198.1 6.4 %convolution_convert_fusion.2 = bf16[4096,768]{1,0:T(8,128)(2,1)} fusion(bf16[384,4096]{1,0:T(8,128)(2,1)S(1)} %bitcast.97, bf16[384,768]{1,0:T(8,128)(2,1)} %get-tuple-element.25), kind=kOutput, calls=%fused_computation.9 | convolution fusion | flops 2419064832 | bytes 10027008 | tf_op jit(solution)/shard_map/dot_general | solution.py:119
  204.5 0.2 reduce-scatter.6.cloned.1.call-start
  204.7 6.6 %convolution_convert_fusion.1 = bf16[4096,768]{1,0:T(8,128)(2,1)} fusion(bf16[384,4096]{1,0:T(8,128)(2,1)S(1)} %bitcast.98, bf16[384,768]{1,0:T(8,128)(2,1)} %get-tuple-element.26), kind=kOutput, calls=%fused_computation.8 | convolution fusion | flops 2419064832 | bytes 10027008 | tf_op jit(solution)/shard_map/dot_general | solution.py:128
  211.6 0.9 copy-done.3
  212.4 9.0 %fusion.5 = f32[384,4096]{1,0:T(8,128)} fusion(bf16[384,768]{1,0:T(8,128)(2,1)S(1)} %copy-done.3, bf16[1,4096,768]{2,1,0:T(8,128)(2,1)} %param.11), kind=kOutput, calls=%fused_computation.16 | convolution fusion | flops 2415919104 | bytes 13172736 | tf_op jit(solution)/shard_map/dot_general | solution.py:107
  221.5 5.0 %add_convert_fusion = bf16[384,4096]{1,0:T(8,128)(2,1)S(1)} fusion(f32[384,4096]{1,0:T(8,128)} %fusion.5, bf16[384,768]{1,0:T(8,128)(2,1)S(1)} %copy-done.6, bf16[1,4096,768]{2,1,0:T(8,128)(2,1)S(1)} %bitcast.105), kind=kOutput, calls=%fused_computation.24 | convolution fusion | flops 2419064832 | bytes 16318464 | tf_op jit(solution)/shard_map/dot_general | solution.py:104
  226.4 1.7 dynamic-slice_bitcast_fusion
  228.2 1.3 collective-permute-start
  229.5 4.0 fusion.15
  233.5 4.7 %all-to-all-start.1 = ((bf16[8,48,4096]{2,1,0:T(8,128)(2,1)}), bf16[8,48,4096]{2,1,0:T(8,128)(2,1)S(1)}, u32[]{:S(2)}, u32[]{:S(2)}) async-start(bf16[8,48,4096]{2,1,0:T(8,128)(2,1)} %bitcast.94), calls=%async_computation.1 | async-start | bytes 6291456 | tf_op jit(solution)/shard_map/all_to_all | solution.py:73
  238.2 4.7 %collective-permute-start.6 = (bf16[1,48,4096]{2,1,0:T(8,128)(2,1)}, bf16[1,48,4096]{2,1,0:T(8,128)(2,1)S(1)}, u32[]{:S(2)}, u32[]{:S(2)}) collective-permute-start(bf16[1,48,4096]{2,1,0:T(8,128)(2,1)} %get-tuple-element.17), channel_id=1, source_target_pairs={{0,7},{1,0},{2,1},{3,2},{4,3},{5,4},{6,5},{7,6},{8,15},{9,8},{10,9... | collective-permute-start | bytes 1179656 | tf_op jit(solution)/shard_map/ppermute | solution.py:25
  242.9 0.6 collective-permute-start.5
  243.5 2.9 collective-permute-start.3
  246.4 1.8 bitcast_dynamic-update-slice_fusion.6
  248.2 87.6 %collective-permute-done.1 = bf16[1,48,4096]{2,1,0:T(8,128)(2,1)S(1)} collective-permute-done((bf16[1,48,4096]{2,1,0:T(8,128)(2,1)}, bf16[1,48,4096]{2,1,0:T(8,128)(2,1)S(1)}, u32[]{:S(2)}, u32[]{:S(2)}) %collective-permute-start.1) | collective-permute-done | bytes 393248 | tf_op jit(solution)/shard_map/ppermute | solution.py:25
  335.8 13.8 %collective-permute-start.2 = (bf16[1,48,4096]{2,1,0:T(8,128)(2,1)}, bf16[1,48,4096]{2,1,0:T(8,128)(2,1)S(1)}, u32[]{:S(2)}, u32[]{:S(2)}) collective-permute-start(bf16[1,48,4096]{2,1,0:T(8,128)(2,1)} %get-tuple-element.21), channel_id=1, source_target_pairs={{0,3},{1,4},{2,5},{3,6},{4,7},{5,0},{6,1},{7,2},{8,11},{9,12},{10,... | collective-permute-start | bytes 1179656 | tf_op jit(solution)/shard_map/ppermute | solution.py:25
  349.7 0.8 bitcast_dynamic-update-slice_fusion.5
  350.5 10.6 %collective-permute-done.2 = bf16[1,48,4096]{2,1,0:T(8,128)(2,1)S(1)} collective-permute-done((bf16[1,48,4096]{2,1,0:T(8,128)(2,1)}, bf16[1,48,4096]{2,1,0:T(8,128)(2,1)S(1)}, u32[]{:S(2)}, u32[]{:S(2)}) %collective-permute-start.2) | collective-permute-done | bytes 393248 | tf_op jit(solution)/shard_map/ppermute | solution.py:25
  361.1 0.8 bitcast_dynamic-update-slice_fusion.4
  361.9 13.4 %collective-permute-done.3 = bf16[1,48,4096]{2,1,0:T(8,128)(2,1)S(1)} collective-permute-done((bf16[1,48,4096]{2,1,0:T(8,128)(2,1)}, bf16[1,48,4096]{2,1,0:T(8,128)(2,1)S(1)}, u32[]{:S(2)}, u32[]{:S(2)}) %collective-permute-start.3) | collective-permute-done | bytes 393248 | tf_op jit(solution)/shard_map/ppermute | solution.py:25
  375.3 0.8 bitcast_dynamic-update-slice_fusion.3
  376.1 0.8 bitcast_dynamic-update-slice_fusion.2
  376.8 0.8 bitcast_dynamic-update-slice_fusion.1
  377.6 0.8 bitcast_dynamic-update-slice_fusion
  378.4 4.4 %gather_fusion.4 = bf16[8,48,4096]{2,1,0:T(8,128)(2,1)} fusion(bf16[8,48,4096]{2,1,0:T(8,128)(2,1)} %bitcast.93, s32[1024]{0:T(1024)S(1)} %pad_clamp_fusion), kind=kCustom, calls=%fused_computation.4 | custom fusion | bytes 6291488 | tf_op jit(solution)/shard_map/gather | solution.py:26
  382.8 7.5 %gather_fusion.5 = bf16[256,4096]{1,0:T(8,128)(2,1)} fusion(bf16[384,4096]{1,0:T(8,128)(2,1)} %bitcast.90, s32[1024]{0:T(1024)S(1)} %pad_clamp_fusion.2), kind=kCustom, calls=%fused_computation.5 | custom fusion | bytes 4195328 | tf_op jit(solution)/shard_map/gather | solution.py:112
  390.4 4.6 %gather.29 = bf16[128,2,4096]{2,1,0:T(2,128)(2,1)} reshape(bf16[256,4096]{1,0:T(8,128)(2,1)} %gather_fusion.5) | data formatting | bytes 4194304 | tf_op jit(solution)/shard_map/gather | solution.py:112
  395.0 7.7 %reduce_sum.35 = bf16[128,4096]{1,0:T(8,128)(2,1)} reduce(bf16[128,2,4096]{2,1,0:T(2,128)(2,1)} %gather.29, bf16[]{:T(256)} %constant.92.clone.1), dimensions={1}, to_apply=%region_5.6 | reduce | flops 524288 | bytes 3145730 | tf_op jit(solution)/shard_map/reduce_sum | solution.py:113
  402.7 3.2 gather_fusion.1
  405.9 5.8 %reshape.159 = f32[128,2,4096]{2,1,0:T(2,128)} reshape(bf16[256,4096]{1,0:T(8,128)(2,1)} %gather_fusion.1) | data formatting | bytes 6291456 | tf_op jit(solution)/shard_map/convert_element_type | solution.py:81
  411.7 9.6 %multiply_reduce_fusion = bf16[128,4096]{1,0:T(8,128)(2,1)} fusion(f32[128,2,4096]{2,1,0:T(2,128)} %reshape.159, f32[128,2]{1,0:T(8,128)S(1)} %copy.14), kind=kLoop, calls=%fused_computation.26 | loop fusion | flops 1572864 | bytes 5243904 | tf_op jit(solution)/shard_map/reduce_sum | solution.py:83
  421.3 2.6 copy.19
  (47 shorter events, 0.2 us)
Async XLA Ops:
  7.2 8.4 %copy-start = (bf16[128,4096]{1,0:T(8,128)(2,1)S(1)}, bf16[128,4096]{1,0:T(8,128)(2,1)}, u32[]{:S(2)}) copy-start(bf16[128,4096]{1,0:T(8,128)(2,1)} %param.13) | copy-start | bytes 3145732
  24.1 7.5 %copy-start.2 = (bf16[128,4096]{1,0:T(8,128)(2,1)S(1)}, bf16[128,4096]{1,0:T(8,128)(2,1)}, u32[]{:S(2)}) copy-start(bf16[128,4096]{1,0:T(8,128)(2,1)} %param.7) | copy-start | bytes 3145732
  24.1 78.2 %all-to-all-start.2 = ((bf16[8,48,4096]{2,1,0:T(8,128)(2,1)}), bf16[8,48,4096]{2,1,0:T(8,128)(2,1)}, u32[]{:S(2)}, u32[]{:S(2)}) async-start(bf16[8,48,4096]{2,1,0:T(8,128)(2,1)} %fusion), calls=%async_computation.2 | async-start | bytes 6291456 | tf_op jit(solution)/shard_map/all_to_all | solution.py:89
  102.4 74.5 %all-to-all-start = ((bf16[8,48,4096]{2,1,0:T(8,128)(2,1)}), bf16[8,48,4096]{2,1,0:T(8,128)(2,1)S(1)}, u32[]{:S(2)}, u32[]{:S(2)}) async-start(bf16[8,48,4096]{2,1,0:T(8,128)(2,1)} %broadcast_select_fusion), calls=%async_computation | async-start | bytes 6291456 | tf_op jit(solution)/shard_map/all_to_all | solution.py:63
  106.0 315.3 %reduce-scatter.8.cloned.1.call-start = ((), (), s32[]{:S(2)}) async-start(), calls=%async_computation.8 | async-start | bytes 7864320 | tf_op jit(solution)/shard_map/reduce_scatter | solution.py:137
  176.9 5.5 %copy-start.7 = (f32[384,768]{1,0:T(8,128)S(1)}, f32[384,768]{1,0:T(8,128)}, u32[]{:S(2)}) copy-start(f32[384,768]{1,0:T(8,128)} %fusion.1) | copy-start | bytes 3538948
  189.2 0.8 copy-start.4
  198.0 225.9 %reduce-scatter.4.cloned.1.call-start = ((), (), s32[]{:S(2)}) async-start(), calls=%async_computation.6 | async-start | bytes 7864320 | tf_op jit(solution)/shard_map/reduce_scatter | solution.py:118
  204.5 219.4 %reduce-scatter.6.cloned.1.call-start = ((), (), s32[]{:S(2)}) async-start(), calls=%async_computation.7 | async-start | bytes 7864320 | tf_op jit(solution)/shard_map/reduce_scatter | solution.py:127
  211.4 1.1 copy-start.3
  211.4 10.0 %slice-start = ((s8[6291456]{0:T(1024)(128)(4,1)}), s8[2097152]{0:T(1024)(128)(4,1)S(1)}, s32[]{:S(2)}) async-start(s8[6291456]{0:T(1024)(128)(4,1)} %bitcast.104), calls=%async_computation.9 | async-start | bytes 4194304
  212.4 9.0 %slice-start.1 = ((s8[6291456]{0:T(1024)(128)(4,1)}), s8[4194304]{0:T(1024)(128)(4,1)S(1)}, s32[]{:S(2)}) async-start(s8[6291456]{0:T(1024)(128)(4,1)} %bitcast.104), calls=%async_computation.10 | async-start | bytes 8388608
  212.4 9.0 %copy-start.6 = (bf16[384,768]{1,0:T(8,128)(2,1)S(1)}, bf16[384,768]{1,0:T(8,128)(2,1)}, u32[]{:S(2)}) copy-start(bf16[384,768]{1,0:T(8,128)(2,1)} %get-tuple-element.25) | copy-start | bytes 1769476
  212.4 17.0 %slice-start.2 = ((s8[6291456]{0:T(1024)(128)(4,1)}), s8[4194304]{0:T(1024)(128)(4,1)S(1)}, s32[]{:S(2)}) async-start(s8[6291456]{0:T(1024)(128)(4,1)} %bitcast.106), calls=%async_computation.11 | async-start | bytes 8388608
  221.4 8.1 %slice-start.3 = ((s8[6291456]{0:T(1024)(128)(4,1)}), s8[2097152]{0:T(1024)(128)(4,1)S(1)}, s32[]{:S(2)}) async-start(s8[6291456]{0:T(1024)(128)(4,1)} %bitcast.106), calls=%async_computation.12 | async-start | bytes 4194304
  226.4 3.1 copy-start.5
  228.2 18.3 %collective-permute-start = (bf16[1,48,4096]{2,1,0:T(8,128)(2,1)}, bf16[1,48,4096]{2,1,0:T(8,128)(2,1)}, u32[]{:S(2)}, u32[]{:S(2)}) collective-permute-start(bf16[1,48,4096]{2,1,0:T(8,128)(2,1)} %get-tuple-element.23), channel_id=1, source_target_pairs={{0,1},{1,2},{2,3},{3,4},{4,5},{5,6},{6,7},{7,0},{8,9},{9,10},{10,1... | collective-permute-start | bytes 1179656 | tf_op jit(solution)/shard_map/ppermute | solution.py:25
  233.5 169.1 %all-to-all-start.1 = ((bf16[8,48,4096]{2,1,0:T(8,128)(2,1)}), bf16[8,48,4096]{2,1,0:T(8,128)(2,1)S(1)}, u32[]{:S(2)}, u32[]{:S(2)}) async-start(bf16[8,48,4096]{2,1,0:T(8,128)(2,1)} %bitcast.94), calls=%async_computation.1 | async-start | bytes 6291456 | tf_op jit(solution)/shard_map/all_to_all | solution.py:73
  238.2 139.4 %collective-permute-start.6 = (bf16[1,48,4096]{2,1,0:T(8,128)(2,1)}, bf16[1,48,4096]{2,1,0:T(8,128)(2,1)S(1)}, u32[]{:S(2)}, u32[]{:S(2)}) collective-permute-start(bf16[1,48,4096]{2,1,0:T(8,128)(2,1)} %get-tuple-element.17), channel_id=1, source_target_pairs={{0,7},{1,0},{2,1},{3,2},{4,3},{5,4},{6,5},{7,6},{8,15},{9,8},{10,9... | collective-permute-start | bytes 1179656 | tf_op jit(solution)/shard_map/ppermute | solution.py:25
  242.9 133.9 %collective-permute-start.5 = (bf16[1,48,4096]{2,1,0:T(8,128)(2,1)}, bf16[1,48,4096]{2,1,0:T(8,128)(2,1)S(1)}, u32[]{:S(2)}, u32[]{:S(2)}) collective-permute-start(bf16[1,48,4096]{2,1,0:T(8,128)(2,1)} %get-tuple-element.18), channel_id=1, source_target_pairs={{0,6},{1,7},{2,0},{3,1},{4,2},{5,3},{6,4},{7,5},{8,14},{9,15},{10,... | collective-permute-start | bytes 1179656 | tf_op jit(solution)/shard_map/ppermute | solution.py:25
  243.5 132.6 %collective-permute-start.4 = (bf16[1,48,4096]{2,1,0:T(8,128)(2,1)}, bf16[1,48,4096]{2,1,0:T(8,128)(2,1)S(1)}, u32[]{:S(2)}, u32[]{:S(2)}) collective-permute-start(bf16[1,48,4096]{2,1,0:T(8,128)(2,1)} %get-tuple-element.19), channel_id=1, source_target_pairs={{0,5},{1,6},{2,7},{3,0},{4,1},{5,2},{6,3},{7,4},{8,13},{9,14},{10,... | collective-permute-start | bytes 1179656 | tf_op jit(solution)/shard_map/ppermute | solution.py:25
  243.5 131.8 %collective-permute-start.3 = (bf16[1,48,4096]{2,1,0:T(8,128)(2,1)}, bf16[1,48,4096]{2,1,0:T(8,128)(2,1)S(1)}, u32[]{:S(2)}, u32[]{:S(2)}) collective-permute-start(bf16[1,48,4096]{2,1,0:T(8,128)(2,1)} %get-tuple-element.20), channel_id=1, source_target_pairs={{0,4},{1,5},{2,6},{3,7},{4,0},{5,1},{6,2},{7,3},{8,12},{9,13},{10,... | collective-permute-start | bytes 1179656 | tf_op jit(solution)/shard_map/ppermute | solution.py:25
  246.4 89.4 %collective-permute-start.1 = (bf16[1,48,4096]{2,1,0:T(8,128)(2,1)}, bf16[1,48,4096]{2,1,0:T(8,128)(2,1)S(1)}, u32[]{:S(2)}, u32[]{:S(2)}) collective-permute-start(bf16[1,48,4096]{2,1,0:T(8,128)(2,1)} %get-tuple-element.22), channel_id=1, source_target_pairs={{0,2},{1,3},{2,4},{3,5},{4,6},{5,7},{6,0},{7,1},{8,10},{9,11},{10,... | collective-permute-start | bytes 1179656 | tf_op jit(solution)/shard_map/ppermute | solution.py:25
  335.8 25.3 %collective-permute-start.2 = (bf16[1,48,4096]{2,1,0:T(8,128)(2,1)}, bf16[1,48,4096]{2,1,0:T(8,128)(2,1)S(1)}, u32[]{:S(2)}, u32[]{:S(2)}) collective-permute-start(bf16[1,48,4096]{2,1,0:T(8,128)(2,1)} %get-tuple-element.21), channel_id=1, source_target_pairs={{0,3},{1,4},{2,5},{3,6},{4,7},{5,0},{6,1},{7,2},{8,11},{9,12},{10,... | collective-permute-start | bytes 1179656 | tf_op jit(solution)/shard_map/ppermute | solution.py:25
  405.9 18.0 %copy-start.1 = (bf16[128,4096]{1,0:T(8,128)(2,1)S(1)}, bf16[128,4096]{1,0:T(8,128)(2,1)}, u32[]{:S(2)}) copy-start(bf16[128,4096]{1,0:T(8,128)(2,1)} %param.13) | copy-start | bytes 3145732
Sparse Core Ops, SparseCore 0:
  198.1 57.4 reduce-scatter.7
  258.9 58.3 reduce-scatter.3
  320.4 58.3 reduce-scatter.5
